TPU v7x, 32 devices: a whole 2x2x4 slice. The times are simulated.
32 devices in a mesh: dp: 16 (over z, y, core), mp: 2 (over x).
Axes of the slice: x: 2, y: 2, z: 4, core: 2. Of those that a mesh axis runs over, the one named last changes fastest.
Arguments:
- tokens: bfloat16 [4096, 2048], P(('dp', 'mp')), may hold values from -6 to 6
- doc_lengths: int32 [16, 6], P('dp'), may hold values from 1 to 128, 256 in all within a row
- cotangent: bfloat16 [4096, 2048], P(('dp', 'mp')), may hold values from -6 to 6
- gain_attn: float32 [2048], replicated, may hold values from 0.1 to 1.9
- gain_mlp: float32 [2048], replicated, may hold values from 0.1 to 1.9
- w_qkv: float32 [2048, 3, 2048], P('dp', None, 'mp'), may hold values from -0.1875 to 0.1875
- w_out: float32 [2048, 2048], P('mp', 'dp'), may hold values from -0.375 to 0.375
- w_gate_up: float32 [2048, 2, 5632], P('dp', None, 'mp'), may hold values from -0.125 to 0.125
- w_down: float32 [5632, 2048], P('mp', 'dp'), may hold values from -0.078125 to 0.078125
Outputs:
- block_out: bfloat16 [4096, 2048], P(('dp', 'mp'))
- input_grad: float32 [4096, 2048], P(('dp', 'mp'))
- grad_w_qkv: float32 [2048, 3, 2048], P('dp', None, 'mp')
- grad_w_out: float32 [2048, 2048], P('mp', 'dp')
- grad_w_gate_up: float32 [2048, 2, 5632], P('dp', None, 'mp')
- grad_w_down: float32 [5632, 2048], P('mp', 'dp')
- grad_gain_attn: float32 [2048], replicated
- grad_gain_mlp: float32 [2048], replicated
Inputs may be any that keep to these rules, and one draw needn't show every extreme that they name: `doc_lengths`: each packed row's 6 lengths sum to 256, and the longest of each row is exactly 128.
All inputs are finite; a program needn't handle non-finite values.
Results may differ from a plain program's by a relative error of at most 0.014.
The roundings to bfloat16 on the way count: a program that leaves them out, or rounds other values in their place, can miss the bound.
Values may be sent and summed in bfloat16 or wider, within the bound.
No kernel may reach another device: no remote copies, remote signals or barrier semaphores. Data moves between devices by JAX's collectives and lax.ppermute only.
A program may use at most 256 MiB of HBM per device.

v0:
```python
import jax
import jax.numpy as jnp
from jax import lax
from jax.sharding import PartitionSpec as P

HD = 128
EPSILON = 1e-05
MASKED = -1e30


def row_layout(lengths, row_len):
    doc_ends = jnp.cumsum(lengths)
    places = jnp.arange(row_len, dtype=jnp.int32)
    segment = jnp.sum((places[:, None] >= doc_ends[None, :]).astype(jnp.int32), axis=1)
    starts = doc_ends - lengths
    chosen = segment[:, None] == jnp.arange(lengths.shape[0], dtype=jnp.int32)[None, :]
    doc_start = jnp.sum(jnp.where(chosen, starts[None, :], 0), axis=1)
    return (segment, places - doc_start, places)


def rotary_tables(offsets, head_size):
    half_size = head_size // 2
    frequency = 10000.0 ** (-2.0 * jnp.arange(half_size, dtype=jnp.float32) / head_size)
    angles = offsets.astype(jnp.float32)[:, None] * frequency[None, :]
    return (jnp.cos(angles), jnp.sin(angles))


def rotate(field, cosine, sine_table):
    half_size = field.shape[-1] // 2
    front_half = field[..., :half_size]
    back_half = field[..., half_size:]
    cos_rows = cosine[:, None, :]
    sin_rows = sine_table[:, None, :]
    return jnp.concatenate(
        [
            front_half * cos_rows - back_half * sin_rows,
            back_half * cos_rows + front_half * sin_rows,
        ],
        axis=-1,
    )


def rotate_back(gradient, cosine, sine_table):
    half_size = gradient.shape[-1] // 2
    front_half = gradient[..., :half_size]
    back_half = gradient[..., half_size:]
    cos_rows = cosine[:, None, :]
    sin_rows = sine_table[:, None, :]
    return jnp.concatenate(
        [
            front_half * cos_rows + back_half * sin_rows,
            back_half * cos_rows - front_half * sin_rows,
        ],
        axis=-1,
    )


def norm_scale(field):
    return lax.rsqrt(jnp.mean(field * field, axis=-1, keepdims=True) + EPSILON)


def norm_back(grad_normed, field, gain_vec):
    inverse = norm_scale(field)
    normed = field * inverse
    scaled = grad_normed * gain_vec
    grad_field = inverse * (scaled - normed * jnp.mean(scaled * normed, axis=-1, keepdims=True))
    return (grad_field, jnp.sum(grad_normed * normed, axis=0))


def masked_scores(query_block, keys_rot, seg_rows, segment, place_rows, places, scale):
    raw_scores = jnp.einsum(
        "qhe,khe->hqk", query_block, keys_rot, preferred_element_type=jnp.float32
    )
    allowed = (seg_rows[:, None] == segment[None, :]) & (places[None, :] <= place_rows[:, None])
    return jnp.where(allowed[None], raw_scores * scale, MASKED)


def scatter_sum(gradient, dimension):
    total = lax.psum_scatter(
        gradient.astype(jnp.bfloat16), "dp", scatter_dimension=dimension, tiled=True
    )
    return total.astype(jnp.float32)


def on_device(tokens, doc_lengths, cotangent, gain_attn, gain_mlp, w_qkv, w_out, w_gate_up, w_down):
    local_rows = tokens.shape[0]
    row_len = local_rows * lax.axis_size("mp")
    segment, offsets, places = row_layout(doc_lengths[0], row_len)
    cosine, sine_table = rotary_tables(offsets, HD)
    scale = HD ** (-0.5)
    block_count = max(1, row_len // 512)
    block_len = row_len // block_count
    block_starts = jnp.arange(block_count, dtype=jnp.int32) * block_len
    masters = (
        w_qkv.astype(jnp.bfloat16),
        w_out.astype(jnp.bfloat16),
        w_gate_up.astype(jnp.bfloat16),
        w_down.astype(jnp.bfloat16),
    )
    w_qkv_all, w_out_all, w_gu_all, w_down_all = (
        lax.all_gather(masters[0], "dp", axis=0, tiled=True),
        lax.all_gather(masters[1], "dp", axis=1, tiled=True),
        lax.all_gather(masters[2], "dp", axis=0, tiled=True),
        lax.all_gather(masters[3], "dp", axis=1, tiled=True),
    )
    resid_in = tokens.astype(jnp.float32)
    normed_attn = (resid_in * norm_scale(resid_in) * gain_attn).astype(jnp.bfloat16)
    attn_rows = lax.all_gather(normed_attn, "mp", axis=0, tiled=True)
    projected = jnp.einsum("td,dce->cte", attn_rows, w_qkv_all, preferred_element_type=jnp.float32)
    local_dim = projected.shape[2]
    local_heads = local_dim // HD
    projected = projected.reshape(3, row_len, local_heads, HD)
    queries = rotate(projected[0], cosine, sine_table).astype(jnp.bfloat16)
    keys_rot = rotate(projected[1], cosine, sine_table).astype(jnp.bfloat16)
    values_low = projected[2].astype(jnp.bfloat16)

    def forward_block(row_start):
        scores = masked_scores(queries, keys_rot, segment, segment, places, places, scale)
        row_max = jnp.max(scores, axis=-1, keepdims=True)
        exp_scores = jnp.exp(scores - row_max)
        denominator = jnp.sum(exp_scores, axis=-1, keepdims=True)
        attn_probs = (exp_scores / denominator).astype(jnp.bfloat16)
        mixed = jnp.einsum(
            "hqk,khe->qhe", attn_probs, values_low, preferred_element_type=jnp.float32
        )
        return (mixed.astype(jnp.bfloat16), (row_max + jnp.log(denominator))[..., 0])

    mixed_blocks, log_total = lax.map(forward_block, block_starts)
    mixed_rows = mixed_blocks.reshape(row_len, local_dim)
    part_rows = mixed_rows
    attn_part = lax.psum_scatter(
        jnp.dot(part_rows, w_out_all, preferred_element_type=jnp.float32),
        "mp",
        scatter_dimension=0,
        tiled=True,
    )
    resid_mid = resid_in + attn_part
    normed_mlp = (resid_mid * norm_scale(resid_mid) * gain_mlp).astype(jnp.bfloat16)
    mlp_rows = lax.all_gather(normed_mlp, "mp", axis=0, tiled=True)
    gate_up = jnp.einsum("td,dcf->ctf", mlp_rows, w_gu_all, preferred_element_type=jnp.float32)
    gate_sig = jax.nn.sigmoid(gate_up[0])
    gate_act = gate_up[0] * gate_sig
    hidden = (gate_act * gate_up[1]).astype(jnp.bfloat16)
    part_rows = hidden
    mlp_part = lax.psum_scatter(
        jnp.dot(part_rows, w_down_all, preferred_element_type=jnp.float32).astype(jnp.bfloat16),
        "mp",
        scatter_dimension=0,
        tiled=True,
    ).astype(jnp.float32)
    block_out = (resid_mid + mlp_part).astype(jnp.bfloat16)
    w_qkv_all, w_out_all, w_gu_all, w_down_all = (
        lax.all_gather(masters[0], "dp", axis=0, tiled=True),
        lax.all_gather(masters[1], "dp", axis=1, tiled=True),
        lax.all_gather(masters[2], "dp", axis=0, tiled=True),
        lax.all_gather(masters[3], "dp", axis=1, tiled=True),
    )
    grad_rows = lax.all_gather(cotangent, "mp", axis=0, tiled=True)
    grad_down = jnp.einsum("tf,td->fd", hidden, grad_rows, preferred_element_type=jnp.float32)
    d_hidden = jnp.einsum("td,fd->tf", grad_rows, w_down_all, preferred_element_type=jnp.float32)
    d_gate = d_hidden * gate_up[1] * gate_sig * (1.0 + gate_up[0] * (1.0 - gate_sig))
    d_up = d_hidden * gate_act
    d_gate_up = jnp.stack([d_gate, d_up]).astype(jnp.bfloat16)
    grad_gate_up = jnp.einsum(
        "td,ctf->dcf", mlp_rows, d_gate_up, preferred_element_type=jnp.float32
    )
    mlp_sums = (grad_gate_up, grad_down)
    part_rows = d_gate_up
    d_normed_mlp = lax.psum_scatter(
        jnp.einsum("ctf,dcf->td", part_rows, w_gu_all, preferred_element_type=jnp.float32),
        "mp",
        scatter_dimension=0,
        tiled=True,
    )
    d_resid_norm, gain_mlp_part = norm_back(d_normed_mlp, resid_mid, gain_mlp)
    d_resid_mid = d_resid_norm + cotangent.astype(jnp.float32)
    attn_grad_rows = lax.all_gather(d_resid_mid.astype(jnp.bfloat16), "mp", axis=0, tiled=True)
    grad_out = jnp.einsum(
        "te,td->ed", mixed_rows, attn_grad_rows, preferred_element_type=jnp.float32
    )
    d_mixed = jnp.einsum("td,ed->te", attn_grad_rows, w_out_all, preferred_element_type=jnp.float32)
    d_mixed = d_mixed.astype(jnp.bfloat16).reshape(row_len, local_heads, HD)

    def backward_block(running, pieces):
        d_keys_sum, d_values_sum = running
        row_start, log_block = pieces
        scores = masked_scores(queries, keys_rot, segment, segment, places, places, scale)
        attn_probs = jnp.exp(scores - log_block[..., None])
        d_probs = jnp.einsum(
            "qhe,khe->hqk", d_mixed, values_low, preferred_element_type=jnp.float32
        )
        row_dot = jnp.sum(attn_probs * d_probs, axis=-1, keepdims=True)
        d_raw = (attn_probs * (d_probs - row_dot) * scale).astype(jnp.bfloat16)
        d_query_block = jnp.einsum(
            "hqk,khe->qhe", d_raw, keys_rot, preferred_element_type=jnp.float32
        )
        d_keys_sum = d_keys_sum + jnp.einsum(
            "hqk,qhe->khe", d_raw, queries, preferred_element_type=jnp.float32
        )
        d_values_sum = d_values_sum + jnp.einsum(
            "hqk,qhe->khe",
            attn_probs.astype(jnp.bfloat16),
            d_mixed,
            preferred_element_type=jnp.float32,
        )
        return ((d_keys_sum, d_values_sum), d_query_block)

    zero_heads = jnp.zeros((row_len, local_heads, HD), jnp.float32)
    (d_keys, d_values), d_query_blocks = lax.scan(
        backward_block, (zero_heads, zero_heads), (block_starts, log_total)
    )
    d_queries = d_query_blocks.reshape(row_len, local_heads, HD)
    d_projected = jnp.stack(
        [
            rotate_back(d_queries, cosine, sine_table),
            rotate_back(d_keys, cosine, sine_table),
            d_values,
        ]
    )
    d_projected = d_projected.astype(jnp.bfloat16).reshape(3, row_len, local_dim)
    grad_qkv = jnp.einsum("td,cte->dce", attn_rows, d_projected, preferred_element_type=jnp.float32)
    part_rows = d_projected
    d_normed_attn = lax.psum_scatter(
        jnp.einsum("cte,dce->td", part_rows, w_qkv_all, preferred_element_type=jnp.float32).astype(
            jnp.bfloat16
        ),
        "mp",
        scatter_dimension=0,
        tiled=True,
    ).astype(jnp.float32)
    d_resid_first, gain_attn_part = norm_back(d_normed_attn, resid_in, gain_attn)
    input_grad = d_resid_mid + d_resid_first
    gain_totals = lax.psum((gain_attn_part, gain_mlp_part), ("dp", "mp"))
    weight_sums = (
        scatter_sum(grad_qkv, 0),
        scatter_sum(grad_out, 1),
        scatter_sum(mlp_sums[0], 0),
        scatter_sum(mlp_sums[1], 1),
    )
    return (
        block_out,
        input_grad,
        weight_sums[0],
        weight_sums[1],
        weight_sums[2],
        weight_sums[3],
        gain_totals[0],
        gain_totals[1],
    )


def solution(mesh):
    return jax.shard_map(
        on_device,
        mesh=mesh,
        in_specs=(
            P(("dp", "mp"), None),
            P("dp", None),
            P(("dp", "mp"), None),
            P(),
            P(),
            P("dp", None, "mp"),
            P("mp", "dp"),
            P("dp", None, "mp"),
            P("mp", "dp"),
        ),
        out_specs=(
            P(("dp", "mp"), None),
            P(("dp", "mp"), None),
            P("dp", None, "mp"),
            P("mp", "dp"),
            P("dp", None, "mp"),
            P("mp", "dp"),
            P(),
            P(),
        ),
        check_vma=False,
    )
```

profile of v0, /device:TPU:0, one launch (start us, length us, event | category | flops | bytes accessed | tf_op | source)
XLA Modules:
  0.0 1241.6 jit_solution(8914130683031569904)
XLA Ops:
  14.1 21.2 %all-gather.9.cloned.1.call-done = bf16[256,2048]{1,0:T(8,128)(2,1)} async-done(((bf16[128,2048]{1,0:T(8,128)(2,1)}), bf16[256,2048]{1,0:T(8,128)(2,1)}) %all-gather.9.cloned.1.call-update) | async-done | bytes 1048592 | tf_op jit(solution)/shard_map/all_gather | solution.py:108
  35.3 103.2 %all-gather.11.cloned.1.call-done = bf16[2048,3,1024]{2,0,1:T(8,128)(2,1)} async-done(((bf16[128,3,1024]{2,0,1:T(8,128)(2,1)}), bf16[2048,3,1024]{2,0,1:T(8,128)(2,1)}) %all-gather.11.cloned.1.call-update) | async-done | bytes 12582928 | tf_op jit(solution)/shard_map/all_gather | solution.py:101
  138.5 6.7 convolution_bitcast_fusion.3
  149.8 42.2 %all-gather.13.cloned.1.call-done = bf16[1024,2048]{1,0:T(8,128)(2,1)} async-done(((bf16[1024,128]{1,0:T(8,128)(2,1)}), bf16[1024,2048]{1,0:T(8,128)(2,1)}) %all-gather.13.cloned.1.call-update) | async-done | bytes 4194320 | tf_op jit(solution)/shard_map/all_gather | solution.py:102
  196.9 30.2 %reduce-scatter.13.cloned.1.call-done = f32[128,2048]{1,0:T(8,128)} async-done(((f32[256,2048]{1,0:T(8,128)}), f32[128,2048]{1,0:T(8,128)}) %reduce-scatter.13.cloned.1.call-update) | async-done | bytes 1048592 | tf_op jit(solution)/shard_map/reduce_scatter | solution.py:131
  236.5 14.6 %all-gather.15.cloned.1.call-done = bf16[256,2048]{1,0:T(8,128)(2,1)} async-done(((bf16[128,2048]{1,0:T(8,128)(2,1)}), bf16[256,2048]{1,0:T(8,128)(2,1)}) %all-gather.15.cloned.1.call-update) | async-done | bytes 1048592 | tf_op jit(solution)/shard_map/all_gather | solution.py:139
  251.1 120.7 %all-gather.17.cloned.1.call-done = bf16[2048,2,2816]{2,0,1:T(8,128)(2,1)} async-done(((bf16[128,2,2816]{2,0,1:T(8,128)(2,1)}), bf16[2048,2,2816]{2,0,1:T(8,128)(2,1)}) %all-gather.17.cloned.1.call-update) | async-done | bytes 23068688 | tf_op jit(solution)/shard_map/all_gather | solution.py:103
  371.8 12.7 %convolution_bitcast_fusion = f32[2,256,2816]{2,1,0:T(8,128)} fusion(bf16[2048,2,2816]{2,0,1:T(8,128)(2,1)} %all-gather.17.cloned.1.call-done, bf16[256,2048]{1,0:T(8,128)(2,1)} %all-gather.15.cloned.1.call-done), kind=kOutput, calls=%fused_computation.4 | convolution fusion | flops 5905580032 | bytes 29884416 | tf_op jit(solution)/shard_map/td,dcf->ctf/dot_general | solution.py:140
  384.4 10.2 all-gather.21.cloned.1.call-done
  394.6 99.7 %all-gather.19.cloned.1.call-done = bf16[2816,2048]{1,0:T(8,128)(2,1)} async-done(((bf16[2816,128]{1,0:T(8,128)(2,1)}), bf16[2816,2048]{1,0:T(8,128)(2,1)}) %all-gather.19.cloned.1.call-update) | async-done | bytes 11534352 | tf_op jit(solution)/shard_map/all_gather | solution.py:104
  494.3 12.4 fusion.18
  506.7 12.5 %convolution_bitcast_fusion.2 = f32[256,2048]{1,0:T(8,128)} fusion(bf16[2048,2,2816]{2,0,1:T(8,128)(2,1)} %all-gather.17.cloned.1.call-done, bf16[1,256,2816]{2,1,0:T(8,128)(2,1)} %get-tuple-element.106, bf16[1,256,2816]{2,1,0:T(8,128)(2,1)} %get-tuple-element.105), kind=kOutput, calls=%fused_computation.16 | convolution fusion | flops 5907021824 | bytes 28049408 | tf_op jit(solution)/shard_map/ctf,dcf->td/dot_general | solution.py:170
  519.3 30.2 %reduce-scatter.17.cloned.1.call-done = f32[128,2048]{1,0:T(8,128)} async-done(((f32[256,2048]{1,0:T(8,128)}), f32[128,2048]{1,0:T(8,128)}) %reduce-scatter.17.cloned.1.call-update) | async-done | bytes 1048592 | tf_op jit(solution)/shard_map/reduce_scatter | solution.py:169
  552.6 21.2 %all-gather.23.cloned.1.call-done = bf16[256,2048]{1,0:T(8,128)(2,1)} async-done(((bf16[128,2048]{1,0:T(8,128)(2,1)}), bf16[256,2048]{1,0:T(8,128)(2,1)}) %all-gather.23.cloned.1.call-update) | async-done | bytes 1048592 | tf_op jit(solution)/shard_map/all_gather | solution.py:177
  601.6 9.4 fusion.2
  611.3 8.4 convolution_convert_fusion.4
  637.9 15.8 %copy.127 = bf16[2816,2048]{0,1:T(8,128)(2,1)} copy(bf16[2816,2048]{1,0:T(8,128)(2,1)} %convolution_convert_fusion.1) | data formatting | bytes 23068672
  655.3 7.4 convolution_convert_fusion.2
  664.5 13.2 %convolution_convert_fusion = bf16[2048,2,2816]{2,0,1:T(8,128)(2,1)} fusion(bf16[1,256,2816]{2,1,0:T(8,128)(2,1)} %get-tuple-element.106, bf16[1,256,2816]{2,1,0:T(8,128)(2,1)S(1)} %copy-done.16, bf16[256,2048]{1,0:T(8,128)(2,1)S(1)} %copy-done.3), kind=kOutput, calls=%fused_computation.1 | convolution fusion | flops 5922881536 | bytes 27000832 | tf_op jit(solution)/shard_map/td,ctf->dcf/dot_general | solution.py:164
  680.2 40.9 %all-reduce = (f32[2048]{0:T(1024)}, f32[2048]{0:T(1024)}) all-reduce(f32[2048]{0:T(1024)S(1)} %get-tuple-element.99, f32[2048]{0:T(1024)S(1)} %get-tuple-element.97), channel_id=1, replica_groups=mesh['dp'=16,'mp'=2] {'dp','mp'}, use_global_device_ids=true, to_apply=%region_19.20 | all-reduce | flops 4096 | bytes 32768 | tf_op jit(solution)/shard_map/psum | solution.py:233
  724.1 7.5 reduce-scatter.25.cloned.1.call-done
  733.5 128.2 %reduce-scatter.27.cloned.1.call-done = bf16[128,2816]{1,0:T(8,128)(2,1)} async-done(((bf16[2048,2816]{1,0:T(8,128)(2,1)}), bf16[128,2816]{1,0:T(8,128)(2,1)}) %reduce-scatter.27.cloned.1.call-update) | async-done | bytes 720912
  864.4 135.4 %reduce-scatter.21.cloned.1.call-done = bf16[128,3,1024]{2,0,1:T(8,128)(2,1)} async-done(((bf16[2048,3,1024]{2,0,1:T(8,128)(2,1)}), bf16[128,3,1024]{2,0,1:T(8,128)(2,1)}) %reduce-scatter.21.cloned.1.call-update) | async-done | bytes 786448 | tf_op jit(solution)/shard_map/reduce_scatter | solution.py:79
  1002.2 228.2 %reduce-scatter.23.cloned.1.call-done = bf16[128,2,2816]{2,0,1:T(8,128)(2,1)} async-done(((bf16[2048,2,2816]{2,0,1:T(8,128)(2,1)}), bf16[128,2,2816]{2,0,1:T(8,128)(2,1)}) %reduce-scatter.23.cloned.1.call-update) | async-done | bytes 1441808 | tf_op jit(solution)/shard_map/reduce_scatter | solution.py:79
  (161 shorter events, 94.9 us)
Async XLA Ops:
  7.2 28.1 %all-gather.9.cloned.1.call-start = ((), (), s32[]{:S(2)}) async-start(), calls=%async_computation.8 | async-start | bytes 1572864 | tf_op jit(solution)/shard_map/all_gather | solution.py:108
  11.1 127.4 %all-gather.11.cloned.1.call-start = ((), (), s32[]{:S(2)}) async-start(), calls=%async_computation.9 | async-start | bytes 13369344 | tf_op jit(solution)/shard_map/all_gather | solution.py:101
  12.2 179.8 %all-gather.13.cloned.1.call-start = ((), (), s32[]{:S(2)}) async-start(), calls=%async_computation.10 | async-start | bytes 4456448 | tf_op jit(solution)/shard_map/all_gather | solution.py:102
  13.0 214.0 %reduce-scatter.13.cloned.1.call-start = ((), (), s32[]{:S(2)}) async-start(), calls=%async_computation.11 | async-start | bytes 3145728 | tf_op jit(solution)/shard_map/reduce_scatter | solution.py:131
  149.8 47.0 %copy-start.17 = (bf16[8,128,256]{2,1,0:T(8,128)(2,1)}, bf16[8,128,256]{2,1,0:T(8,128)(2,1)S(1)}, u32[]{:S(2)}) copy-start(bf16[8,128,256]{2,1,0:T(8,128)(2,1)S(1)} %convolution_convert_fusion.6) | copy-start | bytes 1572868
  196.8 31.9 %copy-start.25 = (f32[2048]{0:T(1024)S(1)}, f32[2048]{0:T(1024)}, u32[]{:S(2)}) copy-start(f32[2048]{0:T(1024)} %param.13) | copy-start | bytes 24580
  196.8 54.3 %all-gather.15.cloned.1.call-start = ((), (), s32[]{:S(2)}) async-start(), calls=%async_computation.12 | async-start | bytes 1572864 | tf_op jit(solution)/shard_map/all_gather | solution.py:139
  228.7 322.5 %copy-start.27 = (f32[128]{0:T(128)}, f32[128]{0:T(128)S(1)}, u32[]{:S(2)}) copy-start(f32[128]{0:T(128)S(1)} %add_rsqrt_fusion) | copy-start | bytes 1540
  229.7 142.1 %all-gather.17.cloned.1.call-start = ((), (), s32[]{:S(2)}) async-start(), calls=%async_computation.13 | async-start | bytes 24510464 | tf_op jit(solution)/shard_map/all_gather | solution.py:103
  232.8 161.8 %all-gather.21.cloned.1.call-start = ((), (), s32[]{:S(2)}) async-start(), calls=%async_computation.16 | async-start | bytes 1572864 | tf_op jit(solution)/shard_map/all_gather | solution.py:158
  233.6 260.7 %all-gather.19.cloned.1.call-start = ((), (), s32[]{:S(2)}) async-start(), calls=%async_computation.14 | async-start | bytes 12255232 | tf_op jit(solution)/shard_map/all_gather | solution.py:104
  235.9 313.6 %reduce-scatter.17.cloned.1.call-start = ((), (), s32[]{:S(2)}) async-start(), calls=%async_computation.17 | async-start | bytes 3145728 | tf_op jit(solution)/shard_map/reduce_scatter | solution.py:169
  519.2 54.6 %all-gather.23.cloned.1.call-start = ((), (), s32[]{:S(2)}) async-start(), calls=%async_computation.18 | async-start | bytes 1572864 | tf_op jit(solution)/shard_map/all_gather | solution.py:177
  552.4 125.4 %reduce-scatter.19.cloned.1.call-start = ((), (), s32[]{:S(2)}) async-start(), calls=%async_computation.19 | async-start | bytes 1572864 | tf_op jit(solution)/shard_map/reduce_scatter | solution.py:223
  601.6 9.7 copy-start.9
  611.0 110.2 %reduce-scatter.15.cloned.1.call-start = ((), (), s32[]{:S(2)}) async-start(), calls=%async_computation.15 | async-start | bytes 1572864 | tf_op jit(solution)/shard_map/reduce_scatter | solution.py:145
  619.8 111.8 %reduce-scatter.25.cloned.1.call-start = ((), (), s32[]{:S(2)}) async-start(), calls=%async_computation.22 | async-start | bytes 4456448
  630.7 231.0 %reduce-scatter.27.cloned.1.call-start = ((), (), s32[]{:S(2)}) async-start(), calls=%async_computation.23 | async-start | bytes 12255232
  653.7 346.0 %reduce-scatter.21.cloned.1.call-start = ((), (), s32[]{:S(2)}) async-start(), calls=%async_computation.20 | async-start | bytes 13369344 | tf_op jit(solution)/shard_map/reduce_scatter | solution.py:79
  662.7 567.7 %reduce-scatter.23.cloned.1.call-start = ((), (), s32[]{:S(2)}) async-start(), calls=%async_computation.21 | async-start | bytes 24510464 | tf_op jit(solution)/shard_map/reduce_scatter | solution.py:79
  677.7 43.5 %copy-start.2 = (f32[128,2048]{1,0:T(8,128)S(1)}, f32[128,2048]{1,0:T(8,128)}, u32[]{:S(2)}) copy-start(f32[128,2048]{1,0:T(8,128)} %reduce-scatter.17.cloned.1.call-done) | copy-start | bytes 3145732
  677.7 43.5 %copy-start.6 = (bf16[128,2048]{1,0:T(8,128)(2,1)S(1)}, bf16[128,2048]{1,0:T(8,128)(2,1)}, u32[]{:S(2)}) copy-start(bf16[128,2048]{1,0:T(8,128)(2,1)} %param.11) | copy-start | bytes 1572868
  677.7 43.5 %copy-start.28 = (f32[128]{0:T(128)S(1)}, f32[128]{0:T(128)}, u32[]{:S(2)}) copy-start(f32[128]{0:T(128)} %copy-done.27) | copy-start | bytes 1540
  677.7 43.5 %copy-start.32 = (f32[128]{0:T(128)S(1)}, f32[128]{0:T(128)}, u32[]{:S(2)}) copy-start(f32[128]{0:T(128)} %copy-done.31) | copy-start | bytes 1540
  (26 other events, 55.8 us)
Sparse Core Ops, SparseCore 0:
  11.3 23.9 all-gather.8
  38.1 100.4 all-gather.10
  141.3 50.7 all-gather.12
  197.0 30.0 reduce-scatter.12
  229.8 21.2 all-gather.14
  253.1 118.6 all-gather.16
  373.3 21.2 all-gather.20
  397.3 96.9 all-gather.18
  519.4 30.0 reduce-scatter.16
  552.5 21.2 all-gather.22
  611.1 20.3 reduce-scatter.18
  634.2 20.3 reduce-scatter.14
  658.5 73.0 reduce-scatter.24
  735.5 126.1 reduce-scatter.26
  865.6 134.1 reduce-scatter.20
  1003.7 226.6 reduce-scatter.22
where the time goes:
time: 1250 us; the launch traced here: 1240 us
  waiting for transfers between devices  994 us (80%)
  matrix products  118 us (9%)
  local copies, waits for them, and re-layouts  46.6 us (4%)
  blocking collectives  40.9 us (3%)
  other arithmetic  26.6 us (2%)
  between operations  14.7 us (1%)
    reduce_scatter x2, waiting for transfers between devices, scatter_sum(): lax.psum_scatter(gradient.astype(jnp.bfloat16), 'dp', scatter_dimension=d...  364 us
    unnamed x18, waiting for transfers between devices  137 us
    all_gather x1, waiting for transfers between devices, on_device(): lax.all_gather(masters[2], 'dp', axis=0, tiled=True)  121 us
    all_gather x1, waiting for transfers between devices, on_device(): lax.all_gather(masters[0], 'dp', axis=0, tiled=True)  103 us
    all_gather x1, waiting for transfers between devices, on_device(): lax.all_gather(masters[3], 'dp', axis=1, tiled=True)  99.7 us
    all_gather x1, waiting for transfers between devices, on_device(): lax.all_gather(masters[1], 'dp', axis=1, tiled=True)  42.2 us
    psum x1, blocking collectives, on_device(): gain_totals = lax.psum((gain_attn_part, gain_mlp_part), ('dp', 'mp'))  40.9 us
    unnamed x79, local copies, waits for them, and re-layouts  40.1 us
  transfers between devices with their start and end apart: 16, of which 14 were waited for; matrix products, arithmetic and copies ran while one was open for 8% of the time, Pallas kernels for 0%

commit v1 on v0

--- a/solution.py
+++ b/solution.py
@@ -2,10 +2,47 @@
 import jax.numpy as jnp
 from jax import lax
 from jax.sharding import PartitionSpec as P
+from jax.lax import axis_index, axis_size, ppermute
 
 HD = 128
 EPSILON = 1e-05
 MASKED = -1e30
+
+
+def layers_all_detail(q_in, d0):
+    lane_axis = "dp"
+    mixed_arr = axis_size(lane_axis)
+    built = axis_index(lane_axis)
+    lanes = []
+    e_now, y1, reply = (mixed_arr, built, q_in.shape[d0])
+    for ii, j0 in enumerate(q_in.shape):
+        lanes.append(j0 * e_now if ii == d0 else j0)
+    all_values = jnp.zeros(lanes, q_in.dtype)
+    outcome_arr = lax.dynamic_update_slice_in_dim(all_values, q_in, y1 * reply, axis=d0)
+    dev = 1
+    earlier = y = q_in
+    while dev < e_now // 2 + 1:
+        blocks_here = []
+        ii = 0
+        while ii < e_now:
+            blocks_here.append((ii, (ii + 1) % e_now))
+            ii = ii + 1
+        earlier = ppermute(earlier, axis_name=lane_axis, perm=blocks_here)
+        outcome_arr = lax.dynamic_update_slice_in_dim(
+            outcome_arr, earlier, (y1 - dev) % e_now * reply, axis=d0
+        )
+        if 2 * dev < e_now:
+            block_list = []
+            ii = 0
+            while ii < e_now:
+                block_list.append((ii, (ii - 1) % e_now))
+                ii += 1
+            y = ppermute(y, axis_name=lane_axis, perm=block_list)
+            outcome_arr = lax.dynamic_update_slice_in_dim(
+                outcome_arr, y, (y1 + dev) % e_now * reply, axis=d0
+            )
+        dev = dev + 1
+    return outcome_arr
 
 
 def row_layout(lengths, row_len):
@@ -100,7 +137,7 @@
     w_qkv_all, w_out_all, w_gu_all, w_down_all = (
         lax.all_gather(masters[0], "dp", axis=0, tiled=True),
         lax.all_gather(masters[1], "dp", axis=1, tiled=True),
-        lax.all_gather(masters[2], "dp", axis=0, tiled=True),
+        layers_all_detail(masters[2], d0=0),
         lax.all_gather(masters[3], "dp", axis=1, tiled=True),
     )
     resid_in = tokens.astype(jnp.float32)

time: 1250 us -> 1360 us (1.088)
  starting transfers between devices: 1.57 us -> 196 us
  waiting for transfers between devices: 994 us -> 811 us
  local copies, waits for them, and re-layouts: 46.6 us -> 133 us
    ppermute x0 -> x15, starting transfers between devices: none -> 195 us  [the longest x8 186 us: layers_all_detail(): earlier = ppermute(earlier, axis_name=lane_axis, perm=blocks_here)]
    all_gather x1, waiting for transfers between devices: 121 us -> 0.01 us  [on_device(): lax.all_gather(masters[2], 'dp', axis=0, tiled=True)]
    all_gather x1, waiting for transfers between devices: 99.7 us -> 0.01 us  [on_device(): lax.all_gather(masters[3], 'dp', axis=1, tiled=True)]
    ppermute x0 -> x15, waiting for transfers between devices: none -> 96.6 us  [the longest x8 92.3 us: layers_all_detail(): earlier = ppermute(earlier, axis_name=lane_axis, perm=blocks_here)]
    unnamed x18, waiting for transfers between devices: 137 us -> 89.8 us
    ppermute x0 -> x15, local copies, waits for them, and re-layouts: none -> 37.9 us  [the longest x8 20.2 us: layers_all_detail(): earlier = ppermute(earlier, axis_name=lane_axis, perm=blocks_here)]
    dynamic_update_slice x0 -> x16, local copies, waits for them, and re-layouts: none -> 32.1 us  [the longest x8 21.7 us: layers_all_detail(): lax.dynamic_update_slice_in_dim(outcome_arr, earlier, (y1 - dev) % e_now...]
    all_gather x1, waiting for transfers between devices: 21.2 us -> 0.02 us  [on_device(): lax.all_gather(d_resid_mid.astype(jnp.bfloat16), 'mp', axis=0, tiled=True)]
  transfers between devices with their start and end apart: 16 -> 31, of which waited for: 14 -> 17; matrix products, arithmetic and copies ran while one was open for 8% -> 19% of each run, Pallas kernels for 0% -> 0%
where the time goes in v1:
time: 1360 us; the launch traced here: 1350 us
  waiting for transfers between devices  811 us (60%)
  starting transfers between devices  196 us (14%)
  local copies, waits for them, and re-layouts  133 us (10%)
  matrix products  124 us (9%)
  blocking collectives  40.1 us (3%)
  other arithmetic  32.7 us (2%)
  between operations  14.7 us (1%)
    reduce_scatter x2, waiting for transfers between devices, scatter_sum(): lax.psum_scatter(gradient.astype(jnp.bfloat16), 'dp', scatter_dimension=d...  362 us
    ppermute x8, starting transfers between devices, layers_all_detail(): earlier = ppermute(earlier, axis_name=lane_axis, perm=blocks_here)  186 us
    all_gather x1, waiting for transfers between devices, on_device(): lax.all_gather(masters[0], 'dp', axis=0, tiled=True)  103 us
    ppermute x8, waiting for transfers between devices, layers_all_detail(): earlier = ppermute(earlier, axis_name=lane_axis, perm=blocks_here)  92.3 us
    unnamed x18, waiting for transfers between devices  89.8 us
    reduce_scatter x1, waiting for transfers between devices, on_device(): lax.psum_scatter(jnp.einsum('ctf,dcf->td', part_rows, w_gu_all, preferred...  47.9 us
    all_gather x1, waiting for transfers between devices, on_device(): lax.all_gather(masters[1], 'dp', axis=1, tiled=True)  42.2 us
    psum x1, blocking collectives, on_device(): gain_totals = lax.psum((gain_attn_part, gain_mlp_part), ('dp', 'mp'))  40.1 us
  transfers between devices with their start and end apart: 31, of which 17 were waited for; matrix products, arithmetic and copies ran while one was open for 19% of the time, Pallas kernels for 0%

profile of v1, /device:TPU:0, one launch (start us, length us, event | category | flops | bytes accessed | tf_op | source)
XLA Modules:
  0.0 1351.5 jit_solution(18258707386945879456)
XLA Ops:
  14.1 21.2 %all-gather.9.cloned.1.call-done = bf16[256,2048]{1,0:T(8,128)(2,1)} async-done(((bf16[128,2048]{1,0:T(8,128)(2,1)}), bf16[256,2048]{1,0:T(8,128)(2,1)}) %all-gather.9.cloned.1.call-update) | async-done | bytes 1048592 | tf_op jit(solution)/shard_map/all_gather | solution.py:145
  35.3 103.2 %all-gather.11.cloned.1.call-done = bf16[2048,3,1024]{2,0,1:T(8,128)(2,1)} async-done(((bf16[128,3,1024]{2,0,1:T(8,128)(2,1)}), bf16[2048,3,1024]{2,0,1:T(8,128)(2,1)}) %all-gather.11.cloned.1.call-update) | async-done | bytes 12582928 | tf_op jit(solution)/shard_map/all_gather | solution.py:138
  149.9 42.2 %all-gather.13.cloned.1.call-done = bf16[1024,2048]{1,0:T(8,128)(2,1)} async-done(((bf16[1024,128]{1,0:T(8,128)(2,1)}), bf16[1024,2048]{1,0:T(8,128)(2,1)}) %all-gather.13.cloned.1.call-update) | async-done | bytes 4194320 | tf_op jit(solution)/shard_map/all_gather | solution.py:139
  196.9 30.2 %reduce-scatter.13.cloned.1.call-done = f32[128,2048]{1,0:T(8,128)} async-done(((f32[256,2048]{1,0:T(8,128)}), f32[128,2048]{1,0:T(8,128)}) %reduce-scatter.13.cloned.1.call-update) | async-done | bytes 1048592 | tf_op jit(solution)/shard_map/reduce_scatter | solution.py:168
  240.3 17.0 %collective-permute-done = bf16[128,2,2816]{2,0,1:T(8,128)(2,1)S(1)} collective-permute-done((bf16[128,2,2816]{2,0,1:T(8,128)(2,1)}, bf16[128,2,2816]{2,0,1:T(8,128)(2,1)S(1)}, u32[]{:S(2)}, u32[]{:S(2)}) %collective-permute-start) | collective-permute-done | bytes 1441824 | tf_op jit(solution)/shard_map/ppermute | solution.py:30
  278.5 31.4 %collective-permute-start.4 = (bf16[128,2,2816]{2,0,1:T(8,128)(2,1)S(1)}, bf16[128,2,2816]{2,0,1:T(8,128)(2,1)S(1)}, u32[]{:S(2)}, u32[]{:S(2)}) collective-permute-start(bf16[128,2,2816]{2,0,1:T(8,128)(2,1)S(1)} %collective-permute-done.2), channel_id=1, source_target_pairs={{0,2},{2,4},{4,6},{6,8},{8,10},{10,12},{12,14},{14,16},{16,18},{18... | collective-permute-start | bytes 4325384 | tf_op jit(solution)/shard_map/ppermute | solution.py:30
  309.9 18.9 %collective-permute-done.4 = bf16[128,2,2816]{2,0,1:T(8,128)(2,1)S(1)} collective-permute-done((bf16[128,2,2816]{2,0,1:T(8,128)(2,1)S(1)}, bf16[128,2,2816]{2,0,1:T(8,128)(2,1)S(1)}, u32[]{:S(2)}, u32[]{:S(2)}) %collective-permute-start.4) | collective-permute-done | bytes 1441824 | tf_op jit(solution)/shard_map/ppermute | solution.py:30
  329.9 14.6 %collective-permute-start.6 = (bf16[128,2,2816]{2,0,1:T(8,128)(2,1)S(1)}, bf16[128,2,2816]{2,0,1:T(8,128)(2,1)}, u32[]{:S(2)}, u32[]{:S(2)}) collective-permute-start(bf16[128,2,2816]{2,0,1:T(8,128)(2,1)S(1)} %collective-permute-done.4), channel_id=1, source_target_pairs={{0,2},{2,4},{4,6},{6,8},{8,10},{10,12},{12,14},{14,16},{16,18},{18... | collective-permute-start | bytes 4325384 | tf_op jit(solution)/shard_map/ppermute | solution.py:30
  356.6 48.8 %collective-permute-start.8 = (bf16[128,2,2816]{2,0,1:T(8,128)(2,1)}, bf16[128,2,2816]{2,0,1:T(8,128)(2,1)}, u32[]{:S(2)}, u32[]{:S(2)}) collective-permute-start(bf16[128,2,2816]{2,0,1:T(8,128)(2,1)} %collective-permute-done.6), channel_id=1, source_target_pairs={{0,2},{2,4},{4,6},{6,8},{8,10},{10,12},{12,14},{14,16},{16,18},{18... | collective-permute-start | bytes 4325384 | tf_op jit(solution)/shard_map/ppermute | solution.py:30
  472.0 32.0 %collective-permute-start.12 = (bf16[128,2,2816]{2,0,1:T(8,128)(2,1)}, bf16[128,2,2816]{2,0,1:T(8,128)(2,1)}, u32[]{:S(2)}, u32[]{:S(2)}) collective-permute-start(bf16[128,2,2816]{2,0,1:T(8,128)(2,1)} %collective-permute-done.10), channel_id=1, source_target_pairs={{0,2},{2,4},{4,6},{6,8},{8,10},{10,12},{12,14},{14,16},{16,18},{18... | collective-permute-start | bytes 4325384 | tf_op jit(solution)/shard_map/ppermute | solution.py:30
  522.2 44.0 %collective-permute-start.14 = (bf16[128,2,2816]{2,0,1:T(8,128)(2,1)}, bf16[128,2,2816]{2,0,1:T(8,128)(2,1)}, u32[]{:S(2)}, u32[]{:S(2)}) collective-permute-start(bf16[128,2,2816]{2,0,1:T(8,128)(2,1)} %collective-permute-done.12), channel_id=1, source_target_pairs={{0,2},{2,4},{4,6},{6,8},{8,10},{10,12},{12,14},{14,16},{16,18},{18... | collective-permute-start | bytes 4325384 | tf_op jit(solution)/shard_map/ppermute | solution.py:30
  579.3 24.7 %collective-permute-done.14 = bf16[128,2,2816]{2,0,1:T(8,128)(2,1)} collective-permute-done((bf16[128,2,2816]{2,0,1:T(8,128)(2,1)}, bf16[128,2,2816]{2,0,1:T(8,128)(2,1)}, u32[]{:S(2)}, u32[]{:S(2)}) %collective-permute-start.14) | collective-permute-done | bytes 1441824 | tf_op jit(solution)/shard_map/ppermute | solution.py:30
  609.3 13.0 convolution_bitcast_fusion
  622.4 12.9 fusion.18
  635.3 12.8 convolution_bitcast_fusion.2
  648.1 47.9 %reduce-scatter.17.cloned.1.call-done = f32[128,2048]{1,0:T(8,128)} async-done(((f32[256,2048]{1,0:T(8,128)}), f32[128,2048]{1,0:T(8,128)}) %reduce-scatter.17.cloned.1.call-update) | async-done | bytes 1048592 | tf_op jit(solution)/shard_map/reduce_scatter | solution.py:206
  708.2 16.1 %copy.210 = bf16[2816,2048]{0,1:T(8,128)(2,1)} copy(bf16[2816,2048]{1,0:T(8,128)(2,1)} %convolution_convert_fusion.1) | data formatting | bytes 23068672
  796.1 12.5 convolution_convert_fusion
  818.0 33.6 %reduce-scatter.27.cloned.1.call-done = bf16[128,2816]{1,0:T(8,128)(2,1)} async-done(((bf16[2048,2816]{1,0:T(8,128)(2,1)}), bf16[128,2816]{1,0:T(8,128)(2,1)}) %reduce-scatter.27.cloned.1.call-update) | async-done | bytes 720912
  856.3 17.7 %reduce-scatter.19.cloned.1.call-done = bf16[128,2048]{1,0:T(8,128)(2,1)} async-done(((bf16[256,2048]{1,0:T(8,128)(2,1)}), bf16[128,2048]{1,0:T(8,128)(2,1)}) %reduce-scatter.19.cloned.1.call-update) | async-done | bytes 524304 | tf_op jit(solution)/shard_map/reduce_scatter | solution.py:260
  875.5 40.1 %all-reduce = (f32[2048]{0:T(1024)}, f32[2048]{0:T(1024)}) all-reduce(f32[2048]{0:T(1024)S(1)} %get-tuple-element.99, f32[2048]{0:T(1024)S(1)} %get-tuple-element.97), channel_id=1, replica_groups=mesh['dp'=16,'mp'=2] {'dp','mp'}, use_global_device_ids=true, to_apply=%region_19.20 | all-reduce | flops 4096 | bytes 32768 | tf_op jit(solution)/shard_map/psum | solution.py:270
  918.6 55.4 %reduce-scatter.25.cloned.1.call-done = bf16[128,1024]{1,0:T(8,128)(2,1)} async-done(((bf16[2048,1024]{1,0:T(8,128)(2,1)}), bf16[128,1024]{1,0:T(8,128)(2,1)}) %reduce-scatter.25.cloned.1.call-update) | async-done | bytes 262160
  975.9 228.5 %reduce-scatter.23.cloned.1.call-done = bf16[128,2,2816]{2,0,1:T(8,128)(2,1)} async-done(((bf16[2048,2,2816]{2,0,1:T(8,128)(2,1)}), bf16[128,2,2816]{2,0,1:T(8,128)(2,1)}) %reduce-scatter.23.cloned.1.call-update) | async-done | bytes 1441808 | tf_op jit(solution)/shard_map/reduce_scatter | solution.py:116
  1208.8 133.4 %reduce-scatter.21.cloned.1.call-done = bf16[128,3,1024]{2,0,1:T(8,128)(2,1)} async-done(((bf16[2048,3,1024]{2,0,1:T(8,128)(2,1)}), bf16[128,3,1024]{2,0,1:T(8,128)(2,1)}) %reduce-scatter.21.cloned.1.call-update) | async-done | bytes 786448 | tf_op jit(solution)/shard_map/reduce_scatter | solution.py:116
  (242 shorter events, 284.5 us)
Async XLA Ops:
  11.1 127.4 %all-gather.11.cloned.1.call-start = ((), (), s32[]{:S(2)}) async-start(), calls=%async_computation.9 | async-start | bytes 13369344 | tf_op jit(solution)/shard_map/all_gather | solution.py:138
  12.2 179.8 %all-gather.13.cloned.1.call-start = ((), (), s32[]{:S(2)}) async-start(), calls=%async_computation.10 | async-start | bytes 4456448 | tf_op jit(solution)/shard_map/all_gather | solution.py:139
  13.0 214.0 %reduce-scatter.13.cloned.1.call-start = ((), (), s32[]{:S(2)}) async-start(), calls=%async_computation.11 | async-start | bytes 3145728 | tf_op jit(solution)/shard_map/reduce_scatter | solution.py:168
  196.8 412.5 %all-gather.15.cloned.1.call-start = ((), (), s32[]{:S(2)}) async-start(), calls=%async_computation.12 | async-start | bytes 1572864 | tf_op jit(solution)/shard_map/all_gather | solution.py:176
  229.7 392.7 %all-gather.19.cloned.1.call-start = ((), (), s32[]{:S(2)}) async-start(), calls=%async_computation.15 | async-start | bytes 1572864 | tf_op jit(solution)/shard_map/all_gather | solution.py:195
  230.2 392.1 %all-gather.17.cloned.1.call-start = ((), (), s32[]{:S(2)}) async-start(), calls=%async_computation.13 | async-start | bytes 12255232 | tf_op jit(solution)/shard_map/all_gather | solution.py:141
  232.6 402.6 %all-gather.21.cloned.1.call-start = ((), (), s32[]{:S(2)}) async-start(), calls=%async_computation.16 | async-start | bytes 24510464 | tf_op jit(solution)/shard_map/all_gather | solution.py:192
  235.8 460.3 %reduce-scatter.17.cloned.1.call-start = ((), (), s32[]{:S(2)}) async-start(), calls=%async_computation.17 | async-start | bytes 3145728 | tf_op jit(solution)/shard_map/reduce_scatter | solution.py:206
  269.2 40.8 %collective-permute-start.3 = (bf16[128,2,2816]{2,0,1:T(8,128)(2,1)S(1)}, bf16[128,2,2816]{2,0,1:T(8,128)(2,1)S(1)}, u32[]{:S(2)}, u32[]{:S(2)}) collective-permute-start(bf16[128,2,2816]{2,0,1:T(8,128)(2,1)S(1)} %collective-permute-done.1), channel_id=1, source_target_pairs={{0,30},{2,0},{4,2},{6,4},{8,6},{10,8},{12,10},{14,12},{16,14},{18,... | collective-permute-start | bytes 4325384 | tf_op jit(solution)/shard_map/ppermute | solution.py:40
  278.5 50.2 %collective-permute-start.4 = (bf16[128,2,2816]{2,0,1:T(8,128)(2,1)S(1)}, bf16[128,2,2816]{2,0,1:T(8,128)(2,1)S(1)}, u32[]{:S(2)}, u32[]{:S(2)}) collective-permute-start(bf16[128,2,2816]{2,0,1:T(8,128)(2,1)S(1)} %collective-permute-done.2), channel_id=1, source_target_pairs={{0,2},{2,4},{4,6},{6,8},{8,10},{10,12},{12,14},{14,16},{16,18},{18... | collective-permute-start | bytes 4325384 | tf_op jit(solution)/shard_map/ppermute | solution.py:30
  344.5 77.9 %collective-permute-start.7 = (bf16[128,2,2816]{2,0,1:T(8,128)(2,1)}, bf16[128,2,2816]{2,0,1:T(8,128)(2,1)}, u32[]{:S(2)}, u32[]{:S(2)}) collective-permute-start(bf16[128,2,2816]{2,0,1:T(8,128)(2,1)} %collective-permute-done.5), channel_id=1, source_target_pairs={{0,30},{2,0},{4,2},{6,4},{8,6},{10,8},{12,10},{14,12},{16,14},{18,... | collective-permute-start | bytes 4325384 | tf_op jit(solution)/shard_map/ppermute | solution.py:40
  356.6 75.0 %collective-permute-start.8 = (bf16[128,2,2816]{2,0,1:T(8,128)(2,1)}, bf16[128,2,2816]{2,0,1:T(8,128)(2,1)}, u32[]{:S(2)}, u32[]{:S(2)}) collective-permute-start(bf16[128,2,2816]{2,0,1:T(8,128)(2,1)} %collective-permute-done.6), channel_id=1, source_target_pairs={{0,2},{2,4},{4,6},{6,8},{8,10},{10,12},{12,14},{14,16},{16,18},{18... | collective-permute-start | bytes 4325384 | tf_op jit(solution)/shard_map/ppermute | solution.py:30
  431.6 40.5 %collective-permute-start.10 = (bf16[128,2,2816]{2,0,1:T(8,128)(2,1)}, bf16[128,2,2816]{2,0,1:T(8,128)(2,1)}, u32[]{:S(2)}, u32[]{:S(2)}) collective-permute-start(bf16[128,2,2816]{2,0,1:T(8,128)(2,1)} %collective-permute-done.8), channel_id=1, source_target_pairs={{0,2},{2,4},{4,6},{6,8},{8,10},{10,12},{12,14},{14,16},{16,18},{18... | collective-permute-start | bytes 4325384 | tf_op jit(solution)/shard_map/ppermute | solution.py:30
  448.1 64.9 %collective-permute-start.11 = (bf16[128,2,2816]{2,0,1:T(8,128)(2,1)}, bf16[128,2,2816]{2,0,1:T(8,128)(2,1)}, u32[]{:S(2)}, u32[]{:S(2)}) collective-permute-start(bf16[128,2,2816]{2,0,1:T(8,128)(2,1)} %collective-permute-done.9), channel_id=1, source_target_pairs={{0,30},{2,0},{4,2},{6,4},{8,6},{10,8},{12,10},{14,12},{16,14},{18,... | collective-permute-start | bytes 4325384 | tf_op jit(solution)/shard_map/ppermute | solution.py:40
  472.0 50.2 %collective-permute-start.12 = (bf16[128,2,2816]{2,0,1:T(8,128)(2,1)}, bf16[128,2,2816]{2,0,1:T(8,128)(2,1)}, u32[]{:S(2)}, u32[]{:S(2)}) collective-permute-start(bf16[128,2,2816]{2,0,1:T(8,128)(2,1)} %collective-permute-done.10), channel_id=1, source_target_pairs={{0,2},{2,4},{4,6},{6,8},{8,10},{10,12},{12,14},{14,16},{16,18},{18... | collective-permute-start | bytes 4325384 | tf_op jit(solution)/shard_map/ppermute | solution.py:30
  513.1 59.7 %collective-permute-start.13 = (bf16[128,2,2816]{2,0,1:T(8,128)(2,1)}, bf16[128,2,2816]{2,0,1:T(8,128)(2,1)}, u32[]{:S(2)}, u32[]{:S(2)}) collective-permute-start(bf16[128,2,2816]{2,0,1:T(8,128)(2,1)} %collective-permute-done.11), channel_id=1, source_target_pairs={{0,30},{2,0},{4,2},{6,4},{8,6},{10,8},{12,10},{14,12},{16,14},{18,... | collective-permute-start | bytes 4325384 | tf_op jit(solution)/shard_map/ppermute | solution.py:40
  522.2 81.9 %collective-permute-start.14 = (bf16[128,2,2816]{2,0,1:T(8,128)(2,1)}, bf16[128,2,2816]{2,0,1:T(8,128)(2,1)}, u32[]{:S(2)}, u32[]{:S(2)}) collective-permute-start(bf16[128,2,2816]{2,0,1:T(8,128)(2,1)} %collective-permute-done.12), channel_id=1, source_target_pairs={{0,2},{2,4},{4,6},{6,8},{8,10},{10,12},{12,14},{14,16},{16,18},{18... | collective-permute-start | bytes 4325384 | tf_op jit(solution)/shard_map/ppermute | solution.py:30
  648.1 76.8 %all-gather.23.cloned.1.call-start = ((), (), s32[]{:S(2)}) async-start(), calls=%async_computation.18 | async-start | bytes 1572864 | tf_op jit(solution)/shard_map/all_gather | solution.py:214
  699.0 152.6 %reduce-scatter.27.cloned.1.call-start = ((), (), s32[]{:S(2)}) async-start(), calls=%async_computation.23 | async-start | bytes 12255232
  724.4 149.6 %reduce-scatter.19.cloned.1.call-start = ((), (), s32[]{:S(2)}) async-start(), calls=%async_computation.19 | async-start | bytes 1572864 | tf_op jit(solution)/shard_map/reduce_scatter | solution.py:260
  774.9 140.7 %reduce-scatter.15.cloned.1.call-start = ((), (), s32[]{:S(2)}) async-start(), calls=%async_computation.14 | async-start | bytes 1572864 | tf_op jit(solution)/shard_map/reduce_scatter | solution.py:182
  783.6 190.4 %reduce-scatter.25.cloned.1.call-start = ((), (), s32[]{:S(2)}) async-start(), calls=%async_computation.22 | async-start | bytes 4456448
  794.5 409.9 %reduce-scatter.23.cloned.1.call-start = ((), (), s32[]{:S(2)}) async-start(), calls=%async_computation.21 | async-start | bytes 24510464 | tf_op jit(solution)/shard_map/reduce_scatter | solution.py:116
  808.7 533.6 %reduce-scatter.21.cloned.1.call-start = ((), (), s32[]{:S(2)}) async-start(), calls=%async_computation.20 | async-start | bytes 13369344 | tf_op jit(solution)/shard_map/reduce_scatter | solution.py:116
  (50 other events, 1676.4 us)
Sparse Core Ops, SparseCore 0:
  11.3 23.9 all-gather.8
  38.1 100.4 all-gather.10
  141.3 50.7 all-gather.12
  197.0 30.0 reduce-scatter.12
  229.8 21.2 all-gather.14
  252.5 21.2 all-gather.18
  276.5 152.9 all-gather.16
  431.7 199.7 all-gather.20
  648.2 47.8 reduce-scatter.16
  699.1 21.2 all-gather.22
  724.5 127.0 reduce-scatter.26
  854.3 19.6 reduce-scatter.18
  876.8 20.5 reduce-scatter.14
  901.2 72.7 reduce-scatter.24
  977.9 226.4 reduce-scatter.22
  1208.3 133.9 reduce-scatter.20
